TPU v7x, 32 devices: a whole 2x2x4 slice. The times are simulated.
32 devices in a mesh: ckpt: 4 (over x, core), wide: 8 (over z, y).
Axes of the slice: x: 2, y: 2, z: 4, core: 2. Of those that a mesh axis runs over, the one named last changes fastest.
Arguments:
- codes: bfloat16 [4, 8, 8192, 1024], P('ckpt', 'wide'), may hold values from -4 to 4
- scales: float32 [4, 8, 8192, 8], P('ckpt', 'wide'), may hold values from 0.5 to 5
- example_ids: int32 [8, 8192], P('wide'), may hold values from 0 to 8191, each once within a row
- targets: bfloat16 [1024, 4096], P('wide'), may hold values from -0.09375 to 0.09375
- owners: int32 [6], replicated, may hold values from 0 to 7, as said below
Outputs:
- scores: float32 [8, 8192, 768], P('wide', 'ckpt')
Inputs may be any that keep to these rules, and one draw needn't show every extreme that they name: `example_ids`: each row is a permutation of the 8192 examples of its group. Distinct owners; owner 0 and owner 8 - 1 are always among them.
All inputs are finite; a program needn't handle non-finite values.
Results may differ from a plain program's by a relative error of at most 0.0029.
Values may be sent and summed in bfloat16 or wider, within the bound.
A program may use at most 192 MiB of HBM per device.

v0:
```python
import jax
import jax.numpy as jnp
from jax import lax
from jax.sharding import PartitionSpec as P


def from_root(shard, axis, root):
    mine = lax.axis_index(axis) == root
    return lax.psum(jnp.where(mine, shard, jnp.zeros_like(shard)), axis)


def fetch(targets, owner, width):
    piece = lax.dynamic_slice_in_dim(targets, lax.axis_index("ckpt") * width, width, 1)
    got = from_root(piece, "wide", owner)
    return lax.all_gather(got, "ckpt", axis=1, tiled=True)


def per_device(codes, scales, example_ids, targets, owners):
    width = codes.shape[-1]
    block = width // scales.shape[-1]
    feats = (codes[0, 0].astype(jnp.float32) * jnp.repeat(scales[0, 0], block, axis=-1)).astype(
        jnp.bfloat16
    )
    ordered = jnp.take(feats, example_ids[0], axis=0)
    rounds = owners.shape[0]
    contract = (((1,), (1,)), ((), ()))
    resident = lax.all_to_all(ordered, "ckpt", split_axis=0, concat_axis=1, tiled=True)
    columns = []
    for step in range(rounds):
        chosen = fetch(targets, owners[step], width)
        columns.append(
            lax.dot_general(resident, chosen, contract, preferred_element_type=jnp.float32)
        )
    result = jnp.concatenate(columns, axis=1)
    scale_factor = 1.0 / lax.axis_size("ckpt")
    return (result * scale_factor)[None]


def solution(mesh):
    return jax.shard_map(
        per_device,
        mesh=mesh,
        in_specs=(
            P("ckpt", "wide", None, None),
            P("ckpt", "wide", None, None),
            P("wide", None),
            P("wide", None),
            P(),
        ),
        out_specs=P("wide", "ckpt", None),
        check_vma=False,
    )
```

profile of v0, /device:TPU:28, one launch (start us, length us, event | category | flops | bytes accessed | tf_op | source)
XLA Modules:
  0.0 416.7 jit_solution(499906623515090295)
XLA Ops:
  6.5 3.5 copy.8
  10.1 0.8 compare_select_fusion
  10.9 10.3 %broadcast_in_dim.15 = f32[8192,8,128]{2,1,0:T(8,128)S(1)} broadcast(f32[8192,8]{1,0:T(8,128)} %copy.8), dimensions={0,1} | broadcast | bytes 33816576 | tf_op jit(solution)/shard_map/broadcast_in_dim | solution.py:21
  21.2 18.0 %fusion = bf16[8192,1024]{1,0:T(8,128)(2,1)} fusion(f32[1024,8,8,128]{3,2,1,0:T(8,128)S(1)} %bitcast.58, bf16[1,1,8192,1024]{3,2,1,0:T(8,128)(2,1)} %param.5), kind=kLoop, calls=%fused_computation.2 | loop fusion | flops 25165824 | bytes 67108864 | tf_op jit(solution)/shard_map/convert_element_type | solution.py:21
  39.1 48.4 %gather_fusion = bf16[8192,1024]{1,0:T(8,128)(2,1)} fusion(bf16[8192,1024]{1,0:T(8,128)(2,1)} %fusion, s32[8192]{0:T(1024)S(1)} %broadcast_clamp_fusion), kind=kCustom, calls=%fused_computation | custom fusion | bytes 33587200 | tf_op jit(solution)/shard_map/jit(_take)/gather | solution.py:24
  87.6 21.9 %copy.9 = bf16[4,2048,1024]{1,2,0:T(8,128)(2,1)} copy(bf16[4,2048,1024]{2,1,0:T(8,128)(2,1)} %bitcast.59) | data formatting | bytes 33554432 | tf_op jit(solution)/shard_map/jit(_take)/gather | solution.py:24
  109.5 0.5 broadcast.55
  110.0 0.7 reduce.3
  110.8 14.2 %broadcast_select_fusion = bf16[4,2048,1024]{1,2,0:T(8,128)(2,1)} fusion(bf16[4,2048,1024]{1,2,0:T(8,128)(2,1)} %copy.9, pred[4,2048]{1,0:T(4,128)(4,1)S(1)} %compare_and_fusion), kind=kLoop, calls=%fused_computation.3 | loop fusion | flops 8388608 | bytes 33562624 | tf_op jit(solution)/shard_map/jit(_take)/select_n | solution.py:24
  125.0 7.1 %all-to-all-start = ((bf16[4,2048,1024]{1,2,0:T(8,128)(2,1)}), bf16[4,2048,1024]{1,2,0:T(8,128)(2,1)}, u32[]{:S(2)}, u32[]{:S(2)}) async-start(bf16[4,2048,1024]{1,2,0:T(8,128)(2,1)} %broadcast_select_fusion), calls=%async_computation | async-start | bytes 33554432 | tf_op jit(solution)/shard_map/all_to_all | solution.py:27
  132.1 0.0 all-reduce.3.cloned.1.call-start
  132.1 0.7 fusion.7
  136.6 2.2 broadcast_select_fusion.1
  138.8 0.0 all-gather.7.cloned.1.call-start
  138.8 89.4 %all-reduce.3.cloned.1.call-done = (bf16[128,1024]{1,0:T(8,128)(2,1)}, bf16[128,1024]{1,0:T(8,128)(2,1)}, bf16[128,1024]{1,0:T(8,128)(2,1)}, bf16[128,1024]{1,0:...) async-done(((bf16[128,1024]{1,0:T(8,128)(2,1)}, bf16[128,1024]{1,0:T(8,128)(2,1)}, bf16[128,1024]{1,0:T(8,128)(2,1)}, bf16[128,1024]{1,0:T(8,128)(2,1)}, ...) | async-done | bytes 1572880 | tf_op jit(solution)/shard_map/psum | solution.py:9
  228.3 0.0 all-gather.9.cloned.1.call-start
  228.3 0.7 all-gather.9.cloned.1.call-update
  229.0 0.5 all-gather.11.cloned.1.call-update
  229.6 0.5 all-gather.13.cloned.1.call-update
  230.2 0.5 all-gather.15.cloned.1.call-update
  230.7 0.2 all-gather.17.cloned.1.call-start
  231.0 0.5 all-gather.17.cloned.1.call-update
  231.5 21.7 %all-gather.7.cloned.1.call-done = bf16[128,4096]{1,0:T(8,128)(2,1)} async-done(((bf16[128,1024]{1,0:T(8,128)(2,1)}), bf16[128,4096]{1,0:T(8,128)(2,1)}) %all-gather.7.cloned.1.call-update) | async-done | bytes 1048592 | tf_op jit(solution)/shard_map/all_gather | solution.py:15
  253.2 86.4 %all-to-all-done = bf16[4,2048,1024]{1,2,0:T(8,128)(2,1)} async-done(((bf16[4,2048,1024]{1,2,0:T(8,128)(2,1)}), bf16[4,2048,1024]{1,2,0:T(8,128)(2,1)}, u32[]{:S(2)}, u32[]{:S(2)}) %all-to-all-start) | async-done | bytes 16777248 | tf_op jit(solution)/shard_map/all_to_all | solution.py:27
  339.6 9.5 %fusion.6 = f32[1,2048,768]{1,2,0:T(8,128)} fusion(bf16[128,4096]{1,0:T(8,128)(2,1)} %all-gather.7.cloned.1.call-done, bf16[2048,4096]{0,1:T(8,128)(2,1)} %bitcast.6), kind=kOutput, calls=%fused_computation.16 | convolution fusion | flops 2147483648 | bytes 18874368 | tf_op jit(solution)/shard_map/dot_general | solution.py:32
  349.0 9.8 %fusion.5 = f32[1,2048,768]{1,2,0:T(8,128)} fusion(f32[1,2048,768]{1,2,0:T(8,128)} %fusion.6, bf16[128,4096]{1,0:T(8,128)(2,1)} %all-gather.9.cloned.1.call-done, bf16[2048,4096]{0,1:T(8,128)(2,1)} %bitcast.6), kind=kOutput, calls=%fused_computation.14 | convolution fusion | flops 2147483648 | bytes 18874368 | tf_op jit(solution)/shard_map/dot_general | solution.py:32
  358.8 9.5 %fusion.4 = f32[1,2048,768]{1,2,0:T(8,128)} fusion(f32[1,2048,768]{1,2,0:T(8,128)} %fusion.5, bf16[128,4096]{1,0:T(8,128)(2,1)} %all-gather.11.cloned.1.call-done, bf16[2048,4096]{0,1:T(8,128)(2,1)} %bitcast.6), kind=kOutput, calls=%fused_computation.12 | convolution fusion | flops 2147483648 | bytes 18874368 | tf_op jit(solution)/shard_map/dot_general | solution.py:32
  368.3 9.4 %fusion.3 = f32[1,2048,768]{1,2,0:T(8,128)} fusion(f32[1,2048,768]{1,2,0:T(8,128)} %fusion.4, bf16[128,4096]{1,0:T(8,128)(2,1)} %all-gather.13.cloned.1.call-done, bf16[2048,4096]{0,1:T(8,128)(2,1)} %bitcast.6), kind=kOutput, calls=%fused_computation.10 | convolution fusion | flops 2147483648 | bytes 18874368 | tf_op jit(solution)/shard_map/dot_general | solution.py:32
  377.7 9.4 %fusion.2 = f32[1,2048,768]{1,2,0:T(8,128)} fusion(f32[1,2048,768]{1,2,0:T(8,128)} %fusion.3, bf16[128,4096]{1,0:T(8,128)(2,1)} %all-gather.15.cloned.1.call-done, bf16[2048,4096]{0,1:T(8,128)(2,1)} %bitcast.6), kind=kOutput, calls=%fused_computation.8 | convolution fusion | flops 2147483648 | bytes 18874368 | tf_op jit(solution)/shard_map/dot_general | solution.py:32
  387.1 9.7 %fusion.1 = f32[1,2048,768]{1,2,0:T(8,128)} fusion(f32[1,2048,768]{1,2,0:T(8,128)} %fusion.2, bf16[128,4096]{1,0:T(8,128)(2,1)} %all-gather.17.cloned.1.call-done, bf16[2048,4096]{0,1:T(8,128)(2,1)} %bitcast.6), kind=kOutput, calls=%fused_computation.6 | convolution fusion | flops 2147483648 | bytes 18874368 | tf_op jit(solution)/shard_map/dot_general | solution.py:32
  396.8 6.6 %broadcast_multiply_fusion = f32[1,2048,768]{1,2,0:T(8,128)} fusion(f32[1,2048,768]{1,2,0:T(8,128)} %fusion.1), kind=kLoop, calls=%fused_computation.4 | loop fusion | flops 1572864 | bytes 12582912 | tf_op jit(solution)/shard_map/mul | solution.py:36
  403.3 6.6 %copy.10 = f32[1,2048,768]{2,1,0:T(8,128)} copy(f32[1,2048,768]{1,2,0:T(8,128)} %broadcast_multiply_fusion) | data formatting | bytes 12582912 | tf_op jit(solution)/shard_map/mul | solution.py:36
  (17 shorter events, 0.2 us)
Async XLA Ops:
  87.6 22.4 %copy-start = (s32[1,8192]{1,0:T(1,128)S(1)}, s32[1,8192]{1,0:T(1,128)}, u32[]{:S(2)}) copy-start(s32[1,8192]{1,0:T(1,128)} %param.7) | copy-start | bytes 98308
  125.0 7.2 %copy-start.1 = (s32[6]{0:T(128)S(1)}, s32[6]{0:T(128)}, u32[]{:S(2)}) copy-start(s32[6]{0:T(128)} %param.9) | copy-start | bytes 76
  125.0 214.6 %all-to-all-start = ((bf16[4,2048,1024]{1,2,0:T(8,128)(2,1)}), bf16[4,2048,1024]{1,2,0:T(8,128)(2,1)}, u32[]{:S(2)}, u32[]{:S(2)}) async-start(bf16[4,2048,1024]{1,2,0:T(8,128)(2,1)} %broadcast_select_fusion), calls=%async_computation | async-start | bytes 33554432 | tf_op jit(solution)/shard_map/all_to_all | solution.py:27
  132.1 96.2 %all-reduce.3.cloned.1.call-start = ((), (), s32[]{:S(2)}) async-start(), calls=%async_computation.7 | async-start | bytes 3145728 | tf_op jit(solution)/shard_map/psum | solution.py:9
  138.8 114.4 %all-gather.7.cloned.1.call-start = ((), (), s32[]{:S(2)}) async-start(), calls=%async_computation.1 | async-start | bytes 1310720 | tf_op jit(solution)/shard_map/all_gather | solution.py:15
  228.3 120.8 %all-gather.9.cloned.1.call-start = ((), (), s32[]{:S(2)}) async-start(), calls=%async_computation.2 | async-start | bytes 1310720 | tf_op jit(solution)/shard_map/all_gather | solution.py:15
  229.0 129.8 %all-gather.11.cloned.1.call-start = ((), (), s32[]{:S(2)}) async-start(), calls=%async_computation.3 | async-start | bytes 1310720 | tf_op jit(solution)/shard_map/all_gather | solution.py:15
  229.6 138.7 %all-gather.13.cloned.1.call-start = ((), (), s32[]{:S(2)}) async-start(), calls=%async_computation.4 | async-start | bytes 1310720 | tf_op jit(solution)/shard_map/all_gather | solution.py:15
  230.2 147.5 %all-gather.15.cloned.1.call-start = ((), (), s32[]{:S(2)}) async-start(), calls=%async_computation.5 | async-start | bytes 1310720 | tf_op jit(solution)/shard_map/all_gather | solution.py:15
  230.7 156.4 %all-gather.17.cloned.1.call-start = ((), (), s32[]{:S(2)}) async-start(), calls=%async_computation.6 | async-start | bytes 1310720 | tf_op jit(solution)/shard_map/all_gather | solution.py:15
Sparse Core Ops, SparseCore 0:
  138.9 89.2 all-reduce.2
  229.8 23.3 all-gather.6
  254.8 22.4 all-gather.8
  278.6 22.4 all-gather.10
  302.5 22.3 all-gather.12
  326.3 18.1 all-gather.14
  346.1 16.6 all-gather.16
where the time goes:
time: 418 us; the launch traced here: 417 us
  waiting for transfers between devices  200 us (48%)
  local copies, waits for them, and re-layouts  91.9 us (22%)
  matrix products  57.2 us (14%)
  other arithmetic  42.4 us (10%)
  between operations  17.3 us (4%)
  starting transfers between devices  7.55 us (2%)
    psum x1, waiting for transfers between devices, from_root(): return lax.psum(jnp.where(mine, shard, jnp.zeros_like(shard)), axis)  89.4 us
    all_to_all x1, waiting for transfers between devices, per_device(): lax.all_to_all(ordered, 'ckpt', split_axis=0, concat_axis=1, tiled=True)  86.4 us
    gather x2, local copies, waits for them, and re-layouts, per_device(): ordered = jnp.take(feats, example_ids[0], axis=0)  70.4 us
    dot_general x6, matrix products, per_device(): lax.dot_general(resident, chosen, contract, preferred_element_type=jnp.fl...  57.2 us
    all_gather x6, waiting for transfers between devices, fetch(): return lax.all_gather(got, 'ckpt', axis=1, tiled=True)  21.7 us
    convert_element_type x1, other arithmetic, per_device(): (codes[0, 0].astype(jnp.float32) * jnp.repeat(scales[0, 0], block, axis=-...  18 us
    select_n x2, other arithmetic, per_device(): ordered = jnp.take(feats, example_ids[0], axis=0)  15 us
    broadcast_in_dim x1, local copies, waits for them, and re-layouts, per_device(): jnp.repeat(scales[0, 0], block, axis=-1)  10.3 us
  transfers between devices with their start and end apart: 8, of which 3 were waited for; matrix products, arithmetic and copies ran while one was open for 12% of the time, Pallas kernels for 0%

commit v1 on v0

--- a/solution.py
+++ b/solution.py
@@ -12,7 +12,9 @@
 def fetch(targets, owner, width):
     piece = lax.dynamic_slice_in_dim(targets, lax.axis_index("ckpt") * width, width, 1)
     got = from_root(piece, "wide", owner)
-    return lax.all_gather(got, "ckpt", axis=1, tiled=True)
+    return jnp.concatenate(
+        lax.all_to_all(jnp.stack([got] * lax.axis_size("ckpt")), "ckpt", 0, 0), axis=1
+    )
 
 
 def per_device(codes, scales, example_ids, targets, owners):

time: 418 us -> 450 us (1.077)
  blocking collectives: 0 us -> 194 us
  waiting for transfers between devices: 200 us -> 16.2 us
  matrix products: 57.2 us -> 74.2 us
  starting transfers between devices: 7.55 us -> 21.5 us
  local copies, waits for them, and re-layouts: 91.9 us -> 78.8 us
    all_to_all x0 -> x1, blocking collectives: none -> 194 us  [per_device(): lax.all_to_all(ordered, 'ckpt', split_axis=0, concat_axis=1, tiled=True)]
    psum x1, waiting for transfers between devices: 89.4 us -> 6.28 us  [from_root(): return lax.psum(jnp.where(mine, shard, jnp.zeros_like(shard)), axis)]
    all_to_all x1 -> x6, waiting for transfers between devices: 86.4 us -> 9.91 us  [fetch(): lax.all_to_all(jnp.stack([got] * lax.axis_size('ckpt')), 'ckpt', 0, 0)]
    gather x2 -> x1, local copies, waits for them, and re-layouts: 70.4 us -> 48.6 us  [per_device(): ordered = jnp.take(feats, example_ids[0], axis=0)]
    all_gather x6 -> x0, waiting for transfers between devices: 21.7 us -> none  [fetch(): return lax.all_gather(got, 'ckpt', axis=1, tiled=True)]
    dot_general x6, matrix products: 57.2 us -> 74.2 us  [per_device(): lax.dot_general(resident, chosen, contract, preferred_element_type=jnp.fl...]
    all_to_all x1 -> x6, starting transfers between devices: 7.1 us -> 21.5 us  [fetch(): lax.all_to_all(jnp.stack([got] * lax.axis_size('ckpt')), 'ckpt', 0, 0)]
    another operation x0 -> x6, local copies, waits for them, and re-layouts: none -> 7.59 us  [fetch(): jnp.stack([got] * lax.axis_size('ckpt'))]
  transfers between devices with their start and end apart: 8 -> 7, of which waited for: 3 -> 7; matrix products, arithmetic and copies ran while one was open for 12% -> 36% of each run, Pallas kernels for 0% -> 0%
where the time goes in v1:
time: 450 us; the launch traced here: 445 us
  blocking collectives  194 us (43%)
  local copies, waits for them, and re-layouts  78.8 us (18%)
  matrix products  74.2 us (16%)
  other arithmetic  42.6 us (9%)
  starting transfers between devices  21.5 us (5%)
  between operations  17.3 us (4%)
  waiting for transfers between devices  16.2 us (4%)
    all_to_all x1, blocking collectives, per_device(): lax.all_to_all(ordered, 'ckpt', split_axis=0, concat_axis=1, tiled=True)  194 us
    dot_general x6, matrix products, per_device(): lax.dot_general(resident, chosen, contract, preferred_element_type=jnp.fl...  74.2 us
    gather x1, local copies, waits for them, and re-layouts, per_device(): ordered = jnp.take(feats, example_ids[0], axis=0)  48.6 us
    all_to_all x6, starting transfers between devices, fetch(): lax.all_to_all(jnp.stack([got] * lax.axis_size('ckpt')), 'ckpt', 0, 0)  21.5 us
    convert_element_type x1, other arithmetic, per_device(): (codes[0, 0].astype(jnp.float32) * jnp.repeat(scales[0, 0], block, axis=-...  18 us
    select_n x2, other arithmetic, per_device(): ordered = jnp.take(feats, example_ids[0], axis=0)  14.3 us
    broadcast_in_dim x1, local copies, waits for them, and re-layouts, per_device(): jnp.repeat(scales[0, 0], block, axis=-1)  10.3 us
    all_to_all x6, waiting for transfers between devices, fetch(): lax.all_to_all(jnp.stack([got] * lax.axis_size('ckpt')), 'ckpt', 0, 0)  9.91 us
  transfers between devices with their start and end apart: 7, of which 7 were waited for; matrix products, arithmetic and copies ran while one was open for 36% of the time, Pallas kernels for 0%

profile of v1, /device:TPU:28, one launch (start us, length us, event | category | flops | bytes accessed | tf_op | source)
XLA Modules:
  0.0 444.6 jit_solution(7888055737200694805)
XLA Ops:
  6.5 1.5 fusion.55
  11.9 2.2 broadcast_select_fusion.1
  14.1 3.5 copy.8
  18.2 1.5 reduce.3
  19.8 10.3 %broadcast_in_dim.15 = f32[8192,8,128]{2,1,0:T(8,128)S(1)} broadcast(f32[8192,8]{1,0:T(8,128)} %copy.8), dimensions={0,1} | broadcast | bytes 33816576 | tf_op jit(solution)/shard_map/broadcast_in_dim | solution.py:23
  30.1 18.0 %fusion = bf16[8192,1024]{1,0:T(8,128)(2,1)} fusion(f32[1024,8,8,128]{3,2,1,0:T(8,128)S(1)} %bitcast.104, bf16[1,1,8192,1024]{3,2,1,0:T(8,128)(2,1)} %param.5), kind=kLoop, calls=%fused_computation.2 | loop fusion | flops 25165824 | bytes 67108864 | tf_op jit(solution)/shard_map/convert_element_type | solution.py:23
  48.1 48.6 %gather_fusion = bf16[8192,1024]{1,0:T(8,128)(2,1)} fusion(bf16[8192,1024]{1,0:T(8,128)(2,1)} %fusion, s32[8192]{0:T(1024)S(1)} %broadcast_clamp_fusion), kind=kCustom, calls=%fused_computation | custom fusion | bytes 33587200 | tf_op jit(solution)/shard_map/jit(_take)/gather | solution.py:26
  96.8 6.3 %all-reduce.3.cloned.1.call-done = (bf16[128,1024]{1,0:T(8,128)(2,1)}, bf16[128,1024]{1,0:T(8,128)(2,1)}, bf16[128,1024]{1,0:T(8,128)(2,1)}, bf16[128,1024]{1,0:...) async-done(((bf16[128,1024]{1,0:T(8,128)(2,1)}, bf16[128,1024]{1,0:T(8,128)(2,1)}, bf16[128,1024]{1,0:T(8,128)(2,1)}, bf16[128,1024]{1,0:T(8,128)(2,1)}, ...) | async-done | bytes 1572880 | tf_op jit(solution)/shard_map/psum | solution.py:9
  103.1 2.0 stack.12
  105.1 3.5 all-to-all-start.1
  108.7 14.2 %broadcast_select_fusion = bf16[4,2048,1024]{2,1,0:T(8,128)(2,1)} fusion(bf16[4,2048,1024]{2,1,0:T(8,128)(2,1)} %bitcast.105, pred[4,2048]{1,0:T(4,128)(4,1)S(1)} %compare_and_fusion), kind=kLoop, calls=%fused_computation.15 | loop fusion | flops 8388608 | bytes 33562624 | tf_op jit(solution)/shard_map/jit(_take)/select_n | solution.py:26
  123.1 194.1 %all_to_all.43 = bf16[4,2048,1024]{2,1,0:T(8,128)(2,1)} all-to-all(bf16[4,2048,1024]{2,1,0:T(8,128)(2,1)} %broadcast_select_fusion), channel_id=1, replica_groups=mesh['ckpt'=4,'wide'=8] {'ckpt'}, dimensions={0} | all-to-all | bytes 33554432 | tf_op jit(solution)/shard_map/all_to_all | solution.py:29
  318.2 3.5 all-to-all-start.2
  321.8 12.4 %fusion.16 = f32[1,2048,768]{1,2,0:T(8,128)} fusion(bf16[4,2048,1024]{2,1,0:T(8,128)(2,1)} %all_to_all.43, bf16[4,128,1024]{2,1,0:T(8,128)(2,1)S(1)} %all-to-all-done.1), kind=kOutput, calls=%fused_computation.18 | convolution fusion | flops 2147483648 | bytes 18874368 | tf_op jit(solution)/shard_map/dot_general | solution.py:34
  334.1 2.0 all-to-all-done.2
  336.2 1.1 stack.14
  337.3 3.7 all-to-all-start.3
  341.0 12.4 %fusion.22 = f32[1,2048,768]{1,2,0:T(8,128)} fusion(f32[1,2048,768]{1,2,0:T(8,128)} %fusion.16, bf16[4,2048,1024]{2,1,0:T(8,128)(2,1)} %all_to_all.43, bf16[4,128,1024]{2,1,0:T(8,128)(2,1)S(1)} %all-to-all-done.2), kind=kOutput, calls=%fused_computation.20 | convolution fusion | flops 2147483648 | bytes 18874368 | tf_op jit(solution)/shard_map/dot_general | solution.py:34
  353.3 1.8 all-to-all-done.3
  355.2 1.1 stack.15
  356.3 3.5 all-to-all-start.4
  359.8 12.4 %fusion.28 = f32[1,2048,768]{1,2,0:T(8,128)} fusion(f32[1,2048,768]{1,2,0:T(8,128)} %fusion.22, bf16[4,2048,1024]{2,1,0:T(8,128)(2,1)} %all_to_all.43, bf16[4,128,1024]{2,1,0:T(8,128)(2,1)S(1)} %all-to-all-done.3), kind=kOutput, calls=%fused_computation.22 | convolution fusion | flops 2147483648 | bytes 18874368 | tf_op jit(solution)/shard_map/dot_general | solution.py:34
  372.2 2.0 all-to-all-done.4
  375.3 3.5 all-to-all-start.5
  378.8 12.4 %fusion.34 = f32[1,2048,768]{1,2,0:T(8,128)} fusion(f32[1,2048,768]{1,2,0:T(8,128)} %fusion.28, bf16[4,2048,1024]{2,1,0:T(8,128)(2,1)} %all_to_all.43, bf16[4,128,1024]{2,1,0:T(8,128)(2,1)S(1)} %all-to-all-done.4), kind=kOutput, calls=%fused_computation.24 | convolution fusion | flops 2147483648 | bytes 18874368 | tf_op jit(solution)/shard_map/dot_general | solution.py:34
  391.2 2.0 all-to-all-done.5
  394.4 3.7 all-to-all-start.6
  398.1 12.4 %fusion.40 = f32[1,2048,768]{1,2,0:T(8,128)} fusion(f32[1,2048,768]{1,2,0:T(8,128)} %fusion.34, bf16[4,2048,1024]{2,1,0:T(8,128)(2,1)} %all_to_all.43, bf16[4,128,1024]{2,1,0:T(8,128)(2,1)S(1)} %all-to-all-done.5), kind=kOutput, calls=%fused_computation.26 | convolution fusion | flops 2147483648 | bytes 18874368 | tf_op jit(solution)/shard_map/dot_general | solution.py:34
  410.5 1.8 all-to-all-done.6
  412.3 12.4 %fusion.46 = f32[1,2048,768]{1,2,0:T(8,128)} fusion(f32[1,2048,768]{1,2,0:T(8,128)} %fusion.40, bf16[4,2048,1024]{2,1,0:T(8,128)(2,1)} %all_to_all.43, bf16[4,128,1024]{2,1,0:T(8,128)(2,1)S(1)} %all-to-all-done.6), kind=kOutput, calls=%fused_computation.28 | convolution fusion | flops 2147483648 | bytes 18874368 | tf_op jit(solution)/shard_map/dot_general | solution.py:34
  424.6 6.6 %broadcast_multiply_fusion = f32[1,2048,768]{1,2,0:T(8,128)} fusion(f32[1,2048,768]{1,2,0:T(8,128)} %fusion.46), kind=kLoop, calls=%fused_computation.16 | loop fusion | flops 1572864 | bytes 12582912 | tf_op jit(solution)/shard_map/mul | solution.py:38
  431.2 6.6 %copy.9 = f32[1,2048,768]{2,1,0:T(8,128)} copy(f32[1,2048,768]{1,2,0:T(8,128)} %broadcast_multiply_fusion) | data formatting | bytes 12582912 | tf_op jit(solution)/shard_map/mul | solution.py:38
  (23 shorter events, 4.2 us)
Async XLA Ops:
  6.5 96.5 %all-reduce.3.cloned.1.call-start = ((), (), s32[]{:S(2)}) async-start(), calls=%async_computation.7 | async-start | bytes 3145728 | tf_op jit(solution)/shard_map/psum | solution.py:9
  30.1 18.0 %copy-start.5 = (s32[1,8192]{1,0:T(1,128)S(1)}, s32[1,8192]{1,0:T(1,128)}, u32[]{:S(2)}) copy-start(s32[1,8192]{1,0:T(1,128)} %param.7) | copy-start | bytes 98308
  105.1 17.9 %all-to-all-start.1 = ((bf16[4,128,1024]{2,1,0:T(8,128)(2,1)}), bf16[4,128,1024]{2,1,0:T(8,128)(2,1)S(1)}, u32[]{:S(2)}, u32[]{:S(2)}) async-start(bf16[4,128,1024]{2,1,0:T(8,128)(2,1)} %stack.12), calls=%async_computation.1 | async-start | bytes 2097152 | tf_op jit(solution)/shard_map/all_to_all | solution.py:16
  122.9 194.2 %copy-start.4 = (bf16[128,1024]{1,0:T(8,128)(2,1)S(1)}, bf16[128,1024]{1,0:T(8,128)(2,1)}, u32[]{:S(2)}) copy-start(bf16[128,1024]{1,0:T(8,128)(2,1)} %get-tuple-element.6) | copy-start | bytes 786436
  317.1 19.0 %copy-start.3 = (bf16[128,1024]{1,0:T(8,128)(2,1)S(1)}, bf16[128,1024]{1,0:T(8,128)(2,1)}, u32[]{:S(2)}) copy-start(bf16[128,1024]{1,0:T(8,128)(2,1)} %get-tuple-element.7) | copy-start | bytes 786436
  318.2 17.9 %all-to-all-start.2 = ((bf16[4,128,1024]{2,1,0:T(8,128)(2,1)}), bf16[4,128,1024]{2,1,0:T(8,128)(2,1)S(1)}, u32[]{:S(2)}, u32[]{:S(2)}) async-start(bf16[4,128,1024]{2,1,0:T(8,128)(2,1)} %stack.13), calls=%async_computation.2 | async-start | bytes 2097152 | tf_op jit(solution)/shard_map/all_to_all | solution.py:16
  334.1 21.1 %copy-start.2 = (bf16[128,1024]{1,0:T(8,128)(2,1)S(1)}, bf16[128,1024]{1,0:T(8,128)(2,1)}, u32[]{:S(2)}) copy-start(bf16[128,1024]{1,0:T(8,128)(2,1)} %get-tuple-element.8) | copy-start | bytes 786436
  337.3 17.9 %all-to-all-start.3 = ((bf16[4,128,1024]{2,1,0:T(8,128)(2,1)}), bf16[4,128,1024]{2,1,0:T(8,128)(2,1)S(1)}, u32[]{:S(2)}, u32[]{:S(2)}) async-start(bf16[4,128,1024]{2,1,0:T(8,128)(2,1)} %stack.14), calls=%async_computation.3 | async-start | bytes 2097152 | tf_op jit(solution)/shard_map/all_to_all | solution.py:16
  353.3 20.9 %copy-start.1 = (bf16[128,1024]{1,0:T(8,128)(2,1)S(1)}, bf16[128,1024]{1,0:T(8,128)(2,1)}, u32[]{:S(2)}) copy-start(bf16[128,1024]{1,0:T(8,128)(2,1)} %get-tuple-element.9) | copy-start | bytes 786436
  356.3 17.9 %all-to-all-start.4 = ((bf16[4,128,1024]{2,1,0:T(8,128)(2,1)}), bf16[4,128,1024]{2,1,0:T(8,128)(2,1)S(1)}, u32[]{:S(2)}, u32[]{:S(2)}) async-start(bf16[4,128,1024]{2,1,0:T(8,128)(2,1)} %stack.15), calls=%async_computation.4 | async-start | bytes 2097152 | tf_op jit(solution)/shard_map/all_to_all | solution.py:16
  372.2 21.1 %copy-start = (bf16[128,1024]{1,0:T(8,128)(2,1)S(1)}, bf16[128,1024]{1,0:T(8,128)(2,1)}, u32[]{:S(2)}) copy-start(bf16[128,1024]{1,0:T(8,128)(2,1)} %get-tuple-element.10) | copy-start | bytes 786436
  375.3 17.9 %all-to-all-start.5 = ((bf16[4,128,1024]{2,1,0:T(8,128)(2,1)}), bf16[4,128,1024]{2,1,0:T(8,128)(2,1)S(1)}, u32[]{:S(2)}, u32[]{:S(2)}) async-start(bf16[4,128,1024]{2,1,0:T(8,128)(2,1)} %stack.16), calls=%async_computation.5 | async-start | bytes 2097152 | tf_op jit(solution)/shard_map/all_to_all | solution.py:16
  394.4 17.9 %all-to-all-start.6 = ((bf16[4,128,1024]{2,1,0:T(8,128)(2,1)}), bf16[4,128,1024]{2,1,0:T(8,128)(2,1)S(1)}, u32[]{:S(2)}, u32[]{:S(2)}) async-start(bf16[4,128,1024]{2,1,0:T(8,128)(2,1)} %stack.17), calls=%async_computation.6 | async-start | bytes 2097152 | tf_op jit(solution)/shard_map/all_to_all | solution.py:16
Sparse Core Ops, SparseCore 0:
  14.2 88.8 all-reduce.2
